TPU v7x, 256 devices: a whole 4x4x8 slice. The times are simulated.
256 devices in a mesh: seq: 32 (over x, z), mlp: 8 (over y, core).
Axes of the slice: x: 4, y: 4, z: 8, core: 2. Of those that a mesh axis runs over, the one named last changes fastest.
Arguments:
- queries: bfloat16 [1024, 2560], P(('seq', 'mlp')), may hold values from -8 to 8
- new_kv: bfloat16 [1024, 512], P(('seq', 'mlp')), may hold values from -5 to 5
- kv_cache: bfloat16 [4352, 128, 512], P(('seq', 'mlp')), may hold values from -4 to 4, as said below
- lengths: int32 [256], replicated, may hold values from 256 to 16384, as said below
- page_table: int32 [256, 128], replicated, may hold values from -1 to 4351, as said below
- residual: bfloat16 [1024, 2560], P('seq', 'mlp'), may hold values from -3 to 3
- out_weight: bfloat16 [2560, 2560], P(None, 'mlp'), may hold values from -0.125 to 0.125
- norm_gain: float32 [2560], replicated, may hold values from 0.1 to 1.9
- gate_weight: bfloat16 [2560, 3840], P(None, 'mlp'), may hold values from -0.125 to 0.125
- up_weight: bfloat16 [2560, 3840], P(None, 'mlp'), may hold values from -0.125 to 0.125
- down_weight: bfloat16 [3840, 2560], P('mlp'), may hold values from -0.09375 to 0.09375
- next_gain: float32 [2560], replicated, may hold values from 0.1 to 1.9
- qkv_weight: bfloat16 [2560, 3072], P(None, 'mlp'), may hold values from -0.125 to 0.125
Outputs:
- attended: bfloat16 [1024, 2560], P(('seq', 'mlp'))
- residual_out: bfloat16 [1024, 2560], P('seq', 'mlp')
- next_qkv: bfloat16 [1024, 3072], P('seq', 'mlp')
Inputs may be any that keep to these rules, and one draw needn't show every extreme that they name: `lengths`: lengths have a heavy tail; at least one request has exactly 16384. page_table[r, p] is a slot exactly for the pages p holding positions max(0, lengths[r] - 2047) to lengths[r] - 1, and -1 elsewhere. Slots d * 17 to d * 17 + 16 lie on device d of seq+mlp. All pages of request r lie in consecutive slots of ONE device, whose mlp index is r modulo 8; a device may hold the pages of several requests or of none. No slot holds two pages; some device of every mlp index has all 17 slots in use. `kv_cache`: unused slots hold arbitrary values.
All inputs are finite; a program needn't handle non-finite values.
Results may differ from a plain program's by a relative error of at most 0.011.
Values may be sent and summed in bfloat16 or wider, within the bound.
No kernel may reach another device: no remote copies, remote signals or barrier semaphores. Data moves between devices by JAX's collectives and lax.ppermute only.
A program may use at most 64 MiB of HBM per device.

v0:
```python
import jax
import jax.numpy as jnp
from jax import lax
from jax.sharding import PartitionSpec as P

WINDOW = 2048
NEG_FILL = -1e30


def combine_parts(first, second):
    first_max, first_sum, first_acc = first
    second_max, second_sum, second_acc = second
    peak = jnp.maximum(first_max, second_max)
    first_factor = jnp.exp(first_max - peak)
    second_factor = jnp.exp(second_max - peak)
    return (
        peak,
        first_sum * first_factor + second_sum * second_factor,
        first_acc * first_factor[..., None] + second_acc * second_factor[..., None],
    )


def rms_norm(values, gain):
    floats = values.astype(jnp.float32)
    scaled = floats * lax.rsqrt(jnp.mean(floats * floats, axis=-1, keepdims=True) + 1e-06)
    return (scaled * gain).astype(jnp.bfloat16)


def shards(
    queries,
    new_kv,
    kv_cache,
    lengths,
    page_table,
    residual,
    out_weight,
    norm_gain,
    gate_weight,
    up_weight,
    down_weight,
    next_gain,
    qkv_weight,
):
    seq_count = lax.axis_size("seq")
    mlp_count = lax.axis_size("mlp")
    seq_place = lax.axis_index("seq")
    device = seq_place * mlp_count + lax.axis_index("mlp")
    slot_count = kv_cache.shape[0]
    page_len = kv_cache.shape[1]
    head_dim = kv_cache.shape[2] // 2
    token_count = queries.shape[0]
    width = queries.shape[1]
    head_count = width // head_dim
    request_total, page_count = page_table.shape
    scale = head_dim ** (-0.5)
    local_slot = page_table - device * slot_count
    inside = (local_slot >= 0) & (local_slot < slot_count)
    target = jnp.where(inside, local_slot, slot_count).reshape(-1)
    owners = jnp.broadcast_to(
        jnp.arange(request_total, dtype=jnp.int32)[:, None], page_table.shape
    ).reshape(-1)
    page_numbers = jnp.broadcast_to(
        jnp.arange(page_count, dtype=jnp.int32)[None, :], page_table.shape
    ).reshape(-1)
    slot_request = jnp.zeros((slot_count,), jnp.int32).at[target].set(owners, mode="drop")
    slot_page = jnp.zeros((slot_count,), jnp.int32).at[target].set(page_numbers, mode="drop")
    slot_used = jnp.zeros((slot_count,), jnp.bool_).at[target].set(True, mode="drop")
    column_rows = lax.all_gather(queries, "seq", axis=0, tiled=True)
    column_queries = column_rows.reshape(seq_count, token_count, head_count, head_dim)
    slot_column = slot_request // mlp_count
    slot_queries = column_queries[slot_column]
    cache_keys = kv_cache[:, :, :head_dim]
    cache_values = kv_cache[:, :, head_dim:]
    scores = (
        jnp.einsum("sqhd,skd->sqhk", slot_queries, cache_keys, preferred_element_type=jnp.float32)
        * scale
    )
    positions = slot_page[:, None] * page_len + jnp.arange(page_len, dtype=jnp.int32)[None, :]
    slot_length = lengths[slot_request]
    offsets = jnp.arange(token_count, dtype=jnp.int32)
    valid = (
        slot_used[:, None, None]
        & (positions[:, None, :] < slot_length[:, None, None])
        & (
            positions[:, None, :]
            >= slot_length[:, None, None] + offsets[None, :, None] - (WINDOW - 1)
        )
    )
    valid = valid[:, :, None, :]
    page_max = jnp.max(jnp.where(valid, scores, NEG_FILL), axis=-1)
    weights = jnp.where(valid, jnp.exp(scores - page_max[..., None]), 0.0)
    page_sum = jnp.sum(weights, axis=-1)
    page_acc = jnp.einsum(
        "sqhk,skd->sqhd",
        weights.astype(jnp.bfloat16),
        cache_values,
        preferred_element_type=jnp.float32,
    )
    member = (slot_column[None, :] == jnp.arange(seq_count, dtype=jnp.int32)[:, None]) & slot_used[
        None, :
    ]
    request_max = jnp.max(jnp.where(member[:, :, None, None], page_max[None], NEG_FILL), axis=1)
    rescale = jnp.exp(page_max - request_max[slot_column])
    member_float = member.astype(jnp.float32)
    request_sum = jnp.einsum(
        "rs,sqh->rqh", member_float, rescale * page_sum, precision=lax.Precision.HIGHEST
    )
    request_acc = jnp.einsum(
        "rs,sqhd->rqhd",
        member_float,
        rescale[..., None] * page_acc,
        precision=lax.Precision.HIGHEST,
    )
    got_max, got_sum, got_acc = (
        lax.all_to_all(request_max, "seq", split_axis=0, concat_axis=0, tiled=True),
        lax.all_to_all(request_sum, "seq", split_axis=0, concat_axis=0, tiled=True),
        lax.all_to_all(request_acc, "seq", split_axis=0, concat_axis=0, tiled=True),
    )
    peak = jnp.max(got_max, axis=0)
    factor = jnp.exp(got_max - peak[None])
    own_part = (
        peak,
        jnp.sum(factor * got_sum, axis=0),
        jnp.sum(factor[..., None] * got_acc, axis=0),
    )
    own_queries = queries.reshape(token_count, head_count, head_dim)
    new_keys = new_kv[:, :head_dim]
    new_values = new_kv[:, head_dim:]
    new_scores = (
        jnp.einsum("qhd,kd->qhk", own_queries, new_keys, preferred_element_type=jnp.float32) * scale
    )
    causal = (offsets[:, None] >= offsets[None, :])[:, None, :]
    new_max = jnp.max(jnp.where(causal, new_scores, NEG_FILL), axis=-1)
    new_weights = jnp.where(causal, jnp.exp(new_scores - new_max[..., None]), 0.0)
    new_sum = jnp.sum(new_weights, axis=-1)
    new_acc = jnp.einsum(
        "qhk,kd->qhd",
        new_weights.astype(jnp.bfloat16),
        new_values,
        preferred_element_type=jnp.float32,
    )
    final_max, final_sum, final_acc = combine_parts(own_part, (new_max, new_sum, new_acc))
    attended = (final_acc / final_sum[..., None]).reshape(token_count, width).astype(jnp.bfloat16)
    attention_out = jnp.dot(
        lax.all_gather(attended, "mlp", axis=0, tiled=True),
        out_weight,
        preferred_element_type=jnp.float32,
    )
    stream = (residual.astype(jnp.float32) + attention_out).astype(jnp.bfloat16)
    whole_stream = lax.all_gather(stream, "mlp", axis=1, tiled=True)
    normed = rms_norm(whole_stream, norm_gain)
    gate = jnp.dot(normed, gate_weight, preferred_element_type=jnp.float32)
    upward = jnp.dot(normed, up_weight, preferred_element_type=jnp.float32)
    hidden = (jax.nn.gelu(gate, approximate=True) * upward).astype(jnp.bfloat16)
    partial_down = jnp.dot(hidden, down_weight, preferred_element_type=jnp.float32)
    column_width = stream.shape[1]
    column_start = lax.axis_index("mlp") * column_width
    down_total = lax.psum(partial_down, "mlp")
    full_after = (whole_stream.astype(jnp.float32) + down_total).astype(jnp.bfloat16)
    shard_after = lax.dynamic_slice_in_dim(full_after, column_start, column_width, 1)
    normed_next = rms_norm(full_after, next_gain)
    next_qkv = jnp.dot(normed_next, qkv_weight, preferred_element_type=jnp.float32).astype(
        jnp.bfloat16
    )
    return (attended, shard_after, next_qkv)


def solution(mesh):
    return jax.shard_map(
        shards,
        mesh=mesh,
        in_specs=(
            P(("seq", "mlp"), None),
            P(("seq", "mlp"), None),
            P(("seq", "mlp"), None, None),
            P(),
            P(),
            P("seq", "mlp"),
            P(None, "mlp"),
            P(),
            P(None, "mlp"),
            P(None, "mlp"),
            P("mlp", None),
            P(),
            P(None, "mlp"),
        ),
        out_specs=(P(("seq", "mlp"), None), P("seq", "mlp"), P("seq", "mlp")),
        check_vma=False,
    )
```

profile of v0, /device:TPU:2, one launch (start us, length us, event | category | flops | bytes accessed | tf_op | source)
XLA Modules:
  0.0 617.3 jit_solution(3208878940347870312)
XLA Ops:
  7.2 1.1 and_select_fusion
  8.5 120.0 %scatter_custom_fusion = s32[17]{0:T(128)S(1)} fusion(s32[32768]{0:T(1024)S(1)} %bitcast.70, s32[32768]{0:T(1024)S(1)} %iota_bitcast_fusion.1, s32[]{:T(128)} %constant.28.clone.1), kind=kCustom, calls=%fused_computation.111 | custom fusion | bytes 72 | tf_op jit(solution)/shard_map/scatter | solution.py:65
  128.5 1.4 gather_fusion
  130.0 120.0 %scatter_custom_fusion.2 = s32[17]{0:T(128)S(1)} fusion(s32[32768]{0:T(1024)S(1)} %bitcast.71, s32[32768]{0:T(1024)S(1)} %iota_bitcast_fusion, s32[]{:T(128)} %constant.28.clone.1), kind=kCustom, calls=%fused_computation.109 | custom fusion | bytes 72 | tf_op jit(solution)/shard_map/scatter | solution.py:66
  250.1 136.5 %scatter_custom_fusion.1 = pred[17]{0:T(512)(128)(4,1)S(1)} fusion(s32[32768]{0:T(1024)S(1)} %bitcast.72, pred[32768]{0:T(1024)(128)(4,1)S(1)} %broadcast.184, pred[]{:T(512)} %constant.20.clone.1), kind=kCustom, calls=%fused_computation.104 | custom fusion | bytes 18 | tf_op jit(solution)/shard_map/scatter | solution.py:67
  386.7 52.5 %all-gather = bf16[32,4,2560]{2,1,0:T(4,128)(2,1)S(1)} all-gather(bf16[1,4,2560]{2,1,0:T(4,128)(2,1)} %bitcast.74), channel_id=1, replica_groups=mesh['seq'=32,'mlp'=8] {'seq'}, dimensions={0}, use_global_device_ids=true | all-gather | bytes 675840 | tf_op jit(solution)/shard_map/all_gather | solution.py:68
  439.3 1.4 reshape.237
  440.7 2.7 gather_fusion.1
  443.4 2.0 select_reduce_fusion
  446.5 0.7 copy.51
  447.2 1.4 gather_fusion.2
  448.9 0.7 copy.58
  449.6 6.7 %all-to-all-start.2 = ((f32[32,4,10]{2,1,0:T(4,128)}), f32[32,4,10]{2,1,0:T(4,128)S(1)}, u32[]{:S(2)}, u32[]{:S(2)}) async-start(f32[32,4,10]{2,1,0:T(4,128)} %copy.58), calls=%async_computation.2 | async-start | bytes 131072 | tf_op jit(solution)/shard_map/all_to_all | solution.py:116
  456.3 2.7 convolution_multiply_fusion
  459.0 6.5 %all-to-all-done.2 = f32[32,4,10]{2,1,0:T(4,128)S(1)} async-done(((f32[32,4,10]{2,1,0:T(4,128)}), f32[32,4,10]{2,1,0:T(4,128)S(1)}, u32[]{:S(2)}, u32[]{:S(2)}) %all-to-all-start.2) | async-done | bytes 5152 | tf_op jit(solution)/shard_map/all_to_all | solution.py:116
  465.4 5.0 all-to-all-start
  470.4 2.3 fusion.11
  472.7 1.9 copy.55
  474.6 4.9 all-to-all-done
  479.6 6.7 %all-to-all-start.1 = ((f32[32,4,10,256]{3,1,2,0:T(4,128)}), f32[32,4,10,256]{3,1,2,0:T(4,128)}, u32[]{:S(2)}, u32[]{:S(2)}) async-start(f32[32,4,10,256]{3,1,2,0:T(4,128)} %copy.55), calls=%async_computation.1 | async-start | bytes 2621440 | tf_op jit(solution)/shard_map/all_to_all | solution.py:117
  487.1 18.4 %all-to-all-done.1 = f32[32,4,10,256]{3,1,2,0:T(4,128)} async-done(((f32[32,4,10,256]{3,1,2,0:T(4,128)}), f32[32,4,10,256]{3,1,2,0:T(4,128)}, u32[]{:S(2)}, u32[]{:S(2)}) %all-to-all-start.1) | async-done | bytes 1310752 | tf_op jit(solution)/shard_map/all_to_all | solution.py:117
  505.4 1.7 multiply_reduce_fusion
  507.4 13.3 %all-gather.1 = bf16[8,4,2560]{2,1,0:T(4,128)(2,1)S(1)} all-gather(bf16[1,4,2560]{2,1,0:T(4,128)(2,1)S(1)} %reshape.292), channel_id=1, replica_groups=mesh['seq'=32,'mlp'=8] {'mlp'}, dimensions={0}, use_global_device_ids=true | all-gather | bytes 184320 | tf_op jit(solution)/shard_map/all_gather | solution.py:145
  520.8 2.0 fusion.10
  522.8 12.8 %all-gather.2 = bf16[8,320,32]{1,2,0:T(8,128)(2,1)S(1)} all-gather(bf16[1,320,32]{1,2,0:T(8,128)(2,1)S(1)} %fusion.10), channel_id=1, replica_groups=mesh['seq'=32,'mlp'=8] {'mlp'}, dimensions={0}, use_global_device_ids=true | all-gather | bytes 184320 | tf_op jit(solution)/shard_map/all_gather | solution.py:150
  536.0 2.5 fusion.74
  538.5 3.8 fusion.9
  542.3 0.6 copy.63
  542.9 63.1 %all-reduce.2.cloned.1.call-done = f32[32,2560]{1,0:T(8,128)} async-done(((f32[32,2560]{1,0:T(8,128)}), f32[32,2560]{1,0:T(8,128)}) %all-reduce.2.cloned.1.call-update) | async-done | bytes 327696 | tf_op jit(solution)/shard_map/psum | solution.py:158
  606.0 1.1 fusion.15
  607.1 0.7 constant_dynamic-slice_fusion
  607.9 2.6 convolution_convert_fusion
  (49 shorter events, 3.4 us)
Async XLA Ops:
  7.2 531.3 %copy-start = (bf16[480,2560]{1,0:T(8,128)(2,1)S(1)}, bf16[480,2560]{1,0:T(8,128)(2,1)}, u32[]{:S(2)}) copy-start(bf16[480,2560]{1,0:T(8,128)(2,1)} %param.23) | copy-start | bytes 7372804
  449.6 15.8 %all-to-all-start.2 = ((f32[32,4,10]{2,1,0:T(4,128)}), f32[32,4,10]{2,1,0:T(4,128)S(1)}, u32[]{:S(2)}, u32[]{:S(2)}) async-start(f32[32,4,10]{2,1,0:T(4,128)} %copy.58), calls=%async_computation.2 | async-start | bytes 131072 | tf_op jit(solution)/shard_map/all_to_all | solution.py:116
  465.4 14.2 %all-to-all-start = ((f32[32,4,10]{2,1,0:T(4,128)}), f32[32,4,10]{2,1,0:T(4,128)S(1)}, u32[]{:S(2)}, u32[]{:S(2)}) async-start(f32[32,4,10]{2,1,0:T(4,128)} %copy.51), calls=%async_computation | async-start | bytes 131072 | tf_op jit(solution)/shard_map/all_to_all | solution.py:115
  474.6 11.7 %copy-start.1 = (bf16[4,2560]{1,0:T(4,128)(2,1)S(1)}, bf16[4,2560]{1,0:T(4,128)(2,1)}, u32[]{:S(2)}) copy-start(bf16[4,2560]{1,0:T(4,128)(2,1)} %param.13) | copy-start | bytes 61444
  474.6 11.7 %copy-start.5 = (bf16[4,512]{1,0:T(4,128)(2,1)S(1)}, bf16[4,512]{1,0:T(4,128)(2,1)}, u32[]{:S(2)}) copy-start(bf16[4,512]{1,0:T(4,128)(2,1)} %param.14) | copy-start | bytes 12292
  479.6 25.8 %all-to-all-start.1 = ((f32[32,4,10,256]{3,1,2,0:T(4,128)}), f32[32,4,10,256]{3,1,2,0:T(4,128)}, u32[]{:S(2)}, u32[]{:S(2)}) async-start(f32[32,4,10,256]{3,1,2,0:T(4,128)} %copy.55), calls=%async_computation.1 | async-start | bytes 2621440 | tf_op jit(solution)/shard_map/all_to_all | solution.py:117
  486.3 34.5 %copy-start.3 = (bf16[32,320]{1,0:T(8,128)(2,1)S(1)}, bf16[32,320]{1,0:T(8,128)(2,1)}, u32[]{:S(2)}) copy-start(bf16[32,320]{1,0:T(8,128)(2,1)} %param.18) | copy-start | bytes 61444
  486.3 119.8 %all-reduce.2.cloned.1.call-start = ((), (), s32[]{:S(2)}) async-start(), calls=%async_computation.3 | async-start | bytes 655360 | tf_op jit(solution)/shard_map/psum | solution.py:158
  520.7 15.2 %copy-start.2 = (f32[2560]{0:T(1024)S(1)}, f32[2560]{0:T(1024)}, u32[]{:S(2)}) copy-start(f32[2560]{0:T(1024)} %param.20) | copy-start | bytes 30724
  538.4 69.4 %copy-start.4 = (f32[2560]{0:T(1024)S(1)}, f32[2560]{0:T(1024)}, u32[]{:S(2)}) copy-start(f32[2560]{0:T(1024)} %param.24) | copy-start | bytes 30724
Sparse Core Ops, SparseCore 0:
  542.4 63.6 all-reduce.1
where the time goes:
time: 618 us; the launch traced here: 617 us
  local copies, waits for them, and re-layouts  389 us (63%)
  waiting for transfers between devices  92.9 us (15%)
  blocking collectives  78.6 us (13%)
  matrix products  18.6 us (3%)
  starting transfers between devices  18.3 us (3%)
  between operations  14.3 us (2%)
    scatter x1, local copies, waits for them, and re-layouts, shards(): jnp.zeros((slot_count,), jnp.bool_).at[target].set(True, mode='drop')  136 us
    scatter x1, local copies, waits for them, and re-layouts, shards(): jnp.zeros((slot_count,), jnp.int32).at[target].set(owners, mode='drop')  120 us
    scatter x1, local copies, waits for them, and re-layouts, shards(): jnp.zeros((slot_count,), jnp.int32).at[target]  120 us
    psum x1, waiting for transfers between devices, shards(): down_total = lax.psum(partial_down, 'mlp')  63.1 us
    all_gather x1, blocking collectives, shards(): column_rows = lax.all_gather(queries, 'seq', axis=0, tiled=True)  52.5 us
    all_to_all x1, waiting for transfers between devices, shards(): lax.all_to_all(request_acc, 'seq', split_axis=0, concat_axis=0, tiled=True)  18.4 us
    all_gather x1, blocking collectives, shards(): lax.all_gather(attended, 'mlp', axis=0, tiled=True)  13.3 us
    all_gather x1, blocking collectives, shards(): whole_stream = lax.all_gather(stream, 'mlp', axis=1, tiled=True)  12.8 us
  transfers between devices with their start and end apart: 4, of which 4 were waited for; matrix products, arithmetic and copies ran while one was open for 1% of the time, Pallas kernels for 0%

commit v1 on v0

--- a/solution.py
+++ b/solution.py
@@ -155,7 +155,7 @@
     partial_down = jnp.dot(hidden, down_weight, preferred_element_type=jnp.float32)
     column_width = stream.shape[1]
     column_start = lax.axis_index("mlp") * column_width
-    down_total = lax.psum(partial_down, "mlp")
+    down_total = jnp.sum(lax.all_gather(partial_down, "mlp"), axis=0)
     full_after = (whole_stream.astype(jnp.float32) + down_total).astype(jnp.bfloat16)
     shard_after = lax.dynamic_slice_in_dim(full_after, column_start, column_width, 1)
     normed_next = rms_norm(full_after, next_gain)

time: 618 us -> 582 us (0.942)
  waiting for transfers between devices: 92.9 us -> 53.8 us
    psum x1 -> x0, waiting for transfers between devices: 63.1 us -> none  [shards(): down_total = lax.psum(partial_down, 'mlp')]
    all_gather x0 -> x1, waiting for transfers between devices: none -> 26.2 us  [shards(): down_total = jnp.sum(lax.all_gather(partial_down, 'mlp'), axis=0)]
  transfers between devices with their start and end apart: 4 -> 4, of which waited for: 4 -> 4; matrix products, arithmetic and copies ran while one was open for 1% -> 2% of each run, Pallas kernels for 0% -> 0%
where the time goes in v1:
time: 582 us; the launch traced here: 580 us
  local copies, waits for them, and re-layouts  389 us (67%)
  blocking collectives  78.6 us (14%)
  waiting for transfers between devices  53.8 us (9%)
  starting transfers between devices  19 us (3%)
  matrix products  18.6 us (3%)
  between operations  14.3 us (2%)
  other arithmetic  6.5 us (1%)
    scatter x1, local copies, waits for them, and re-layouts, shards(): jnp.zeros((slot_count,), jnp.bool_).at[target].set(True, mode='drop')  136 us
    scatter x1, local copies, waits for them, and re-layouts, shards(): jnp.zeros((slot_count,), jnp.int32).at[target].set(owners, mode='drop')  120 us
    scatter x1, local copies, waits for them, and re-layouts, shards(): jnp.zeros((slot_count,), jnp.int32).at[target]  120 us
    all_gather x1, blocking collectives, shards(): column_rows = lax.all_gather(queries, 'seq', axis=0, tiled=True)  52.5 us
    all_gather x1, waiting for transfers between devices, shards(): down_total = jnp.sum(lax.all_gather(partial_down, 'mlp'), axis=0)  26.2 us
    all_to_all x1, waiting for transfers between devices, shards(): lax.all_to_all(request_acc, 'seq', split_axis=0, concat_axis=0, tiled=True)  18.7 us
    all_gather x1, blocking collectives, shards(): lax.all_gather(attended, 'mlp', axis=0, tiled=True)  13.3 us
    all_gather x1, blocking collectives, shards(): whole_stream = lax.all_gather(stream, 'mlp', axis=1, tiled=True)  12.8 us
  transfers between devices with their start and end apart: 4, of which 4 were waited for; matrix products, arithmetic and copies ran while one was open for 2% of the time, Pallas kernels for 0%

profile of v1, /device:TPU:2, one launch (start us, length us, event | category | flops | bytes accessed | tf_op | source)
XLA Modules:
  0.0 579.8 jit_solution(6181970287313349444)
XLA Ops:
  7.2 1.1 and_select_fusion
  8.5 120.0 %scatter_custom_fusion = s32[17]{0:T(128)S(1)} fusion(s32[32768]{0:T(1024)S(1)} %bitcast.75, s32[32768]{0:T(1024)S(1)} %iota_bitcast_fusion.1, s32[]{:T(128)} %constant.28.clone.1), kind=kCustom, calls=%fused_computation.111 | custom fusion | bytes 72 | tf_op jit(solution)/shard_map/scatter | solution.py:65
  128.5 1.4 gather_fusion
  130.0 120.0 %scatter_custom_fusion.2 = s32[17]{0:T(128)S(1)} fusion(s32[32768]{0:T(1024)S(1)} %bitcast.76, s32[32768]{0:T(1024)S(1)} %iota_bitcast_fusion, s32[]{:T(128)} %constant.28.clone.1), kind=kCustom, calls=%fused_computation.109 | custom fusion | bytes 72 | tf_op jit(solution)/shard_map/scatter | solution.py:66
  250.1 136.5 %scatter_custom_fusion.1 = pred[17]{0:T(512)(128)(4,1)S(1)} fusion(s32[32768]{0:T(1024)S(1)} %bitcast.77, pred[32768]{0:T(1024)(128)(4,1)S(1)} %broadcast.184, pred[]{:T(512)} %constant.20.clone.1), kind=kCustom, calls=%fused_computation.104 | custom fusion | bytes 18 | tf_op jit(solution)/shard_map/scatter | solution.py:67
  386.8 52.5 %all-gather.1 = bf16[32,4,2560]{2,1,0:T(4,128)(2,1)S(1)} all-gather(bf16[1,4,2560]{2,1,0:T(4,128)(2,1)} %bitcast.79), channel_id=1, replica_groups=mesh['seq'=32,'mlp'=8] {'seq'}, dimensions={0}, use_global_device_ids=true | all-gather | bytes 675840 | tf_op jit(solution)/shard_map/all_gather | solution.py:68
  439.4 1.4 reshape.237
  440.8 2.7 gather_fusion.1
  443.5 2.0 select_reduce_fusion
  446.0 0.7 copy.51
  446.8 6.7 %all-to-all-start = ((f32[32,4,10]{2,1,0:T(4,128)}), f32[32,4,10]{2,1,0:T(4,128)S(1)}, u32[]{:S(2)}, u32[]{:S(2)}) async-start(f32[32,4,10]{2,1,0:T(4,128)} %copy.51), calls=%async_computation | async-start | bytes 131072 | tf_op jit(solution)/shard_map/all_to_all | solution.py:115
  453.4 1.5 gather_fusion.2
  455.4 2.7 convolution_multiply_fusion
  458.3 0.7 copy.58
  459.0 3.3 all-to-all-done
  462.3 6.5 %all-to-all-start.2 = ((f32[32,4,10]{2,1,0:T(4,128)}), f32[32,4,10]{2,1,0:T(4,128)S(1)}, u32[]{:S(2)}, u32[]{:S(2)}) async-start(f32[32,4,10]{2,1,0:T(4,128)} %copy.58), calls=%async_computation.2 | async-start | bytes 131072 | tf_op jit(solution)/shard_map/all_to_all | solution.py:116
  468.8 2.3 fusion.11
  471.2 1.9 copy.55
  473.1 5.6 all-to-all-done.2
  478.7 5.7 all-to-all-start.1
  485.2 18.7 %all-to-all-done.1 = f32[32,4,10,256]{3,1,2,0:T(4,128)} async-done(((f32[32,4,10,256]{3,1,2,0:T(4,128)}), f32[32,4,10,256]{3,1,2,0:T(4,128)}, u32[]{:S(2)}, u32[]{:S(2)}) %all-to-all-start.1) | async-done | bytes 1310752 | tf_op jit(solution)/shard_map/all_to_all | solution.py:117
  503.9 1.7 multiply_reduce_fusion
  506.0 13.3 %all-gather.2 = bf16[8,4,2560]{2,1,0:T(4,128)(2,1)S(1)} all-gather(bf16[1,4,2560]{2,1,0:T(4,128)(2,1)S(1)} %reshape.293), channel_id=1, replica_groups=mesh['seq'=32,'mlp'=8] {'mlp'}, dimensions={0}, use_global_device_ids=true | all-gather | bytes 184320 | tf_op jit(solution)/shard_map/all_gather | solution.py:145
  519.3 2.0 fusion.10
  521.4 12.8 %all-gather.3 = bf16[8,320,32]{1,2,0:T(8,128)(2,1)S(1)} all-gather(bf16[1,320,32]{1,2,0:T(8,128)(2,1)S(1)} %fusion.10), channel_id=1, replica_groups=mesh['seq'=32,'mlp'=8] {'mlp'}, dimensions={0}, use_global_device_ids=true | all-gather | bytes 184320 | tf_op jit(solution)/shard_map/all_gather | solution.py:150
  534.5 2.5 fusion.74
  537.0 3.8 fusion.9
  540.8 0.6 copy.63
  541.4 26.2 %all-gather.6.cloned.1.call-done = f32[256,2560]{1,0:T(8,128)} async-done(((f32[32,2560]{1,0:T(8,128)}), f32[256,2560]{1,0:T(8,128)}) %all-gather.6.cloned.1.call-update) | async-done | bytes 2621456 | tf_op jit(solution)/shard_map/all_gather | solution.py:158
  567.6 1.9 reduce_sum.68
  569.7 0.7 constant_dynamic-slice_fusion
  570.4 2.6 convolution_convert_fusion
  (50 shorter events, 3.5 us)
Async XLA Ops:
  7.2 529.8 %copy-start = (bf16[480,2560]{1,0:T(8,128)(2,1)S(1)}, bf16[480,2560]{1,0:T(8,128)(2,1)}, u32[]{:S(2)}) copy-start(bf16[480,2560]{1,0:T(8,128)(2,1)} %param.23) | copy-start | bytes 7372804
  446.8 15.5 %all-to-all-start = ((f32[32,4,10]{2,1,0:T(4,128)}), f32[32,4,10]{2,1,0:T(4,128)S(1)}, u32[]{:S(2)}, u32[]{:S(2)}) async-start(f32[32,4,10]{2,1,0:T(4,128)} %copy.51), calls=%async_computation | async-start | bytes 131072 | tf_op jit(solution)/shard_map/all_to_all | solution.py:115
  462.3 16.4 %all-to-all-start.2 = ((f32[32,4,10]{2,1,0:T(4,128)}), f32[32,4,10]{2,1,0:T(4,128)S(1)}, u32[]{:S(2)}, u32[]{:S(2)}) async-start(f32[32,4,10]{2,1,0:T(4,128)} %copy.58), calls=%async_computation.2 | async-start | bytes 131072 | tf_op jit(solution)/shard_map/all_to_all | solution.py:116
  473.1 11.4 %copy-start.1 = (bf16[4,2560]{1,0:T(4,128)(2,1)S(1)}, bf16[4,2560]{1,0:T(4,128)(2,1)}, u32[]{:S(2)}) copy-start(bf16[4,2560]{1,0:T(4,128)(2,1)} %param.13) | copy-start | bytes 61444
  473.1 11.4 %copy-start.5 = (bf16[4,512]{1,0:T(4,128)(2,1)S(1)}, bf16[4,512]{1,0:T(4,128)(2,1)}, u32[]{:S(2)}) copy-start(bf16[4,512]{1,0:T(4,128)(2,1)} %param.14) | copy-start | bytes 12292
  478.7 25.3 %all-to-all-start.1 = ((f32[32,4,10,256]{3,1,2,0:T(4,128)}), f32[32,4,10,256]{3,1,2,0:T(4,128)}, u32[]{:S(2)}, u32[]{:S(2)}) async-start(f32[32,4,10,256]{3,1,2,0:T(4,128)} %copy.55), calls=%async_computation.1 | async-start | bytes 2621440 | tf_op jit(solution)/shard_map/all_to_all | solution.py:117
  484.4 34.9 %copy-start.3 = (bf16[32,320]{1,0:T(8,128)(2,1)S(1)}, bf16[32,320]{1,0:T(8,128)(2,1)}, u32[]{:S(2)}) copy-start(bf16[32,320]{1,0:T(8,128)(2,1)} %param.18) | copy-start | bytes 61444
  484.4 83.2 %all-gather.6.cloned.1.call-start = ((), (), s32[]{:S(2)}) async-start(), calls=%async_computation.3 | async-start | bytes 2949120 | tf_op jit(solution)/shard_map/all_gather | solution.py:158
  519.3 15.2 %copy-start.2 = (f32[2560]{0:T(1024)S(1)}, f32[2560]{0:T(1024)}, u32[]{:S(2)}) copy-start(f32[2560]{0:T(1024)} %param.20) | copy-start | bytes 30724
  540.8 29.6 %copy-start.4 = (f32[2560]{0:T(1024)S(1)}, f32[2560]{0:T(1024)}, u32[]{:S(2)}) copy-start(f32[2560]{0:T(1024)} %param.24) | copy-start | bytes 30724
Sparse Core Ops, SparseCore 0:
  540.9 26.6 all-gather.5
